TPU v7x, 32 devices: a whole 2x2x4 slice. The times are simulated.
32 devices in a mesh: grp: 8 (over y, x, core), head: 4 (over z).
Axes of the slice: x: 2, y: 2, z: 4, core: 2. Of those that a mesh axis runs over, the one named last changes fastest.
Arguments:
- q_nope: bfloat16 [4, 64, 128, 128], P(None, 'grp', 'head'), may hold values from -6 to 6
- q_rope: bfloat16 [4, 64, 128, 64], P(None, 'grp', 'head'), may hold values from -512 to 512
- w_absorb_k: bfloat16 [128, 128, 512], P('head'), may hold values from -0.5 to 0.5
- w_absorb_v: bfloat16 [128, 512, 128], P('head'), may hold values from -0.25 to 0.25
- latent_cache: bfloat16 [64, 1024, 576], P(('grp', 'head')), may hold values from -4 to 4
- new_latent: bfloat16 [4, 64, 576], P(None, ('grp', 'head')), may hold values from -6 to 6
- lengths: int32 [64], replicated, may hold values from 128 to 1020, as said below
- moves: int32 [4, 1], P('head'), may hold values from 1 to 7
Outputs:
- attended: bfloat16 [4, 64, 128, 128], P(None, 'grp', 'head')
Inputs may be any that keep to these rules, and one draw needn't show every extreme that they name: lengths[r] counts the live rows of latent_cache[r]; its later rows up to 1024 are padding that no query reads.
All inputs are finite; a program needn't handle non-finite values.
Results may differ from a plain program's by a relative error of at most 0.0077.
Values may be sent and summed in bfloat16 or wider, within the bound.
A program may use at most 64 MiB of HBM per device.

v0:
```python
import functools
import math

import jax
import jax.numpy as jnp
from jax import lax
from jax.experimental import pallas as pl
from jax.experimental.pallas import tpu as pltpu
from jax.sharding import PartitionSpec as P

PAIR = 2
EXTRA = 128
LANES = 128
YARN_GAIN = (0.1 * math.log(40.0) + 1.0) ** 2
MESH = pl.DeviceIdType.MESH


def lane(c):
    return slice(c * LANES, (c + 1) * LANES)


def rounded(value):
    return value.astype(jnp.bfloat16)


def wide(value):
    return value.astype(jnp.float32)


def kernel(
    groups, columns, scale,
    length_ref, move_ref, nope_hbm, rope_hbm, fresh_hbm, wk_hbm, wv_hbm, cache_hbm,
    out_ref,
    nope_ref, rope_ref, fresh_ref, entry_sem,
    wk, wv, keys, newer, local_sem,
    rows_in, rows_mid, rows_out,
    lat_send, lat_recv, rot_send, rot_recv, back_send, back_recv,
    mine, moved, mine_key, moved_key, home, home_recv, shift_of, shift_mine,
    lat_ss, lat_rs, rot_ss, rot_rs, back_ss, back_rs,
    mine_ss, mine_rs, key_ss, key_rs, home_ss, home_rs, shift_ss, shift_rs,
):
    steps, _, heads, _ = nope_ref.shape
    holders, entries, capacity = cache_hbm.shape
    latent = wk.shape[2]
    rope = entries - latent
    movers = move_ref.shape[1]
    spans = steps // PAIR
    total = capacity + EXTRA
    cuts = lat_send.shape[2]
    cut = heads // cuts
    rank = lax.axis_index("grp")
    column = lax.axis_index("head")
    parts = wk.shape[0] // local_part(heads)
    part = local_part(heads)

    wk_copies = [
        pltpu.make_async_copy(
            wk_hbm.at[pl.ds(n * part, part)], wk.at[pl.ds(n * part, part)], local_sem.at[n]
        )
        for n in range(parts)
    ]
    key_copies = [
        pltpu.make_async_copy(
            cache_hbm.at[k], keys.at[k], local_sem.at[parts + k]
        )
        for k in range(holders)
    ]
    wv_copy = pltpu.make_async_copy(wv_hbm, wv, local_sem.at[parts + holders])
    entry_copies = [
        pltpu.make_async_copy(src, dst, entry_sem.at[n])
        for n, (src, dst) in enumerate(
            ((rope_hbm, rope_ref), (nope_hbm, nope_ref), (fresh_hbm, fresh_ref))
        )
    ]
    for copy in entry_copies + wk_copies:
        copy.start()

    def at_column(e):
        return (rank, lax.rem(column + e + columns, columns))

    def at_group(d):
        return (lax.rem(rank + d + groups, groups), column)

    def remote(src, dst, send, recv, target):
        return pltpu.make_async_remote_copy(
            src_ref=src, dst_ref=dst, send_sem=send, recv_sem=recv,
            device_id=target, device_id_type=MESH,
        )

    barrier = pltpu.get_barrier_semaphore()
    for e in range(1, columns):
        pl.semaphore_signal(barrier, inc=1, device_id=at_column(e), device_id_type=MESH)
    for d in range(1, groups):
        pl.semaphore_signal(barrier, inc=1, device_id=at_group(d), device_id_type=MESH)

    def slot(e, k):
        return lax.rem(column + e, columns) * holders + k

    def turned(span, e, k):
        return jnp.concatenate(
            [rope_ref[span * PAIR + s, slot(e, k)] for s in range(PAIR)], axis=1
        )

    for copy in entry_copies:
        copy.wait()
    for k in range(movers):
        for e in range(columns):
            for s in range(PAIR):
                mine[k, s, e] = nope_ref[PAIR + s, slot(e, k)]
            mine[k, PAIR, e] = turned(1, e, k)
        shift_mine[k] = jnp.full(shift_mine.shape[1:], move_ref[0, k], jnp.int32)
        shift_of[0, k] = jnp.full(shift_mine.shape[1:], move_ref[0, k], jnp.int32)
    row = lax.broadcasted_iota(jnp.int32, (16, entries), 0)

    def fresh_rows(k):
        found = jnp.zeros((16, entries), jnp.float32)
        for j in range(steps):
            found = jnp.where(row == j, wide(fresh_ref[j])[k : k + 1], found)
        return found

    for k in range(holders):
        newer[k] = jnp.zeros((EXTRA, entries), jnp.bfloat16)
        newer[k, 0:16] = rounded(fresh_rows(k))
    for k in range(movers):
        mine_key[k] = rounded(fresh_rows(k))
    pl.semaphore_wait(barrier, columns - 1 + groups - 1)

    shift_copies = [
        remote(shift_mine, shift_of.at[e], shift_ss.at[e], shift_rs.at[e], at_column(-e))
        for e in range(1, columns)
    ]
    mine_copies = [
        remote(mine, moved.at[d - 1], mine_ss.at[d - 1], mine_rs.at[d - 1], at_group(-d))
        for d in range(1, groups)
    ]
    newer_copies = [
        remote(mine_key, moved_key.at[d - 1], key_ss.at[d - 1], key_rs.at[d - 1], at_group(-d))
        for d in range(1, groups)
    ]
    for copy in shift_copies + mine_copies + newer_copies:
        copy.start()

    def lat_copy(u, e, c):
        return remote(
            lat_send.at[u, e, c], lat_recv.at[u, e, c], lat_ss.at[u, e, c], lat_rs.at[u, e, c],
            at_column(e),
        )

    def rot_copy(u, e):
        return remote(
            rot_send.at[u, e], rot_recv.at[u, e], rot_ss.at[u, e], rot_rs.at[u, e], at_column(e)
        )

    def back_copy(u, e):
        return remote(
            back_send.at[u, e], back_recv.at[u, e], back_ss.at[u, e], back_rs.at[u, e],
            at_column(-e),
        )

    low, high = jnp.int32(0), jnp.int32(columns - 1)
    upward, downward = [], []
    for _ in range(columns - 1):
        take_high = high - column >= column - low
        target = jnp.where(take_high, high, low)
        upward.append(lax.rem(target - column + columns, columns))
        downward.append(lax.rem(column - target + columns, columns))
        high = jnp.where(take_high, high - 1, high)
        low = jnp.where(take_high, low, low + 1)

    def chosen(e, k, options):
        found = wide(options(0))
        for d in range(2, groups):
            is_it = shift_of[e, k, 0:1, 0:1] == d
            found = jnp.where(is_it, wide(options(d - 1)), found)
        return found

    unit_rows = columns * PAIR * heads

    def place(k, e, s):
        return ((k * columns + e) * PAIR + s) * heads

    def turn(span, k):
        u = span * holders + k
        for e in range(columns):
            if span and k < movers:
                pair = rounded(chosen(e, k, lambda n: moved[n, k, PAIR, e]))
            else:
                pair = turned(span, e, k)
            if e:
                rot_send[u, e] = pair
            else:
                rot_recv[u, 0] = pair
        for e in upward:
            rot_copy(u, e).start()

    def absorb(members, first):
        count = len(members) * columns * PAIR
        for m, (span, k) in enumerate(members):
            for e in range(columns):
                for s in range(PAIR):
                    if span and k < movers:
                        value = chosen(e, k, lambda n: moved[n, k, s, e])
                    else:
                        value = wide(nope_ref[span * PAIR + s, slot(e, k)])
                    rows_in[pl.ds(place(m, e, s), heads)] = value
        for n in range(parts):
            if first:
                wk_copies[n].wait()

            def head(i, carry):
                picked = rounded(rows_in[pl.ds(i, count, stride=heads)])
                result = jnp.dot(picked, wk[i], preferred_element_type=jnp.float32)
                for c in range(latent // LANES):
                    rows_mid[c, pl.ds(i, count, stride=heads)] = result[:, lane(c)]
                return carry

            lax.fori_loop(n * part, (n + 1) * part, head, 0, unroll=True)
            if (n + 1) % (parts // cuts):
                continue
            c = n // (parts // cuts)
            for m, (span, k) in enumerate(members):
                u = span * holders + k
                for e in range(columns):
                    value = jnp.concatenate(
                        [
                            jnp.concatenate(
                                [
                                    rounded(rows_mid[l, pl.ds(place(m, e, s) + c * cut, cut)])
                                    for l in range(latent // LANES)
                                ],
                                axis=1,
                            )
                            for s in range(PAIR)
                        ],
                        axis=0,
                    )
                    if e:
                        lat_send[u, e, c] = value
                    else:
                        lat_recv[u, 0, c] = value
                for e in upward:
                    lat_copy(u, e, c).start()

    settled = [(0, k) for k in range(holders)] + [(1, k) for k in range(movers, holders)]
    moving = [(1, k) for k in range(movers)]
    for span, k in settled:
        turn(span, k)
    absorb(settled, True)
    for copy in key_copies:
        copy.start()
    for copy in shift_copies:
        copy.wait()
    for copy in mine_copies + newer_copies:
        copy.wait()
    for span, k in moving:
        turn(span, k)
    absorb(moving, False)
    wv_copy.start()
    for copy in key_copies:
        copy.wait()
    for k in range(movers):
        later = chosen(0, k, lambda n: moved_key[n, k])
        newer[k, 0:16] = rounded(jnp.where(row < PAIR, wide(newer[k, 0:16]), later))

    at_key = lax.broadcasted_iota(jnp.int32, (1, total), 1)
    at_row = lax.broadcasted_iota(jnp.int32, (unit_rows, 1), 0)
    within = lax.rem(lax.div(at_row, cut), PAIR)

    def unit(u, carry):
        span = lax.div(u, holders)
        k = lax.rem(u, holders)
        for e in range(1, columns):
            for c in range(cuts):
                lat_copy(u, e, c).wait_recv()
            rot_copy(u, e).wait_recv()
        live = length_ref[(rank * columns + column) * holders + k]
        token = jnp.where(at_key < capacity, steps, at_key - capacity)
        token = jnp.where(at_key < live, -1, token)
        nt = (((1,), (1,)), ((), ()))
        queries = lat_recv[u].reshape(unit_rows, latent)
        turns = rot_recv[u]
        turns = jnp.concatenate(
            [
                turns[e][c * cut : (c + 1) * cut, s * rope : (s + 1) * rope]
                for e in range(columns)
                for c in range(cuts)
                for s in range(PAIR)
            ],
            axis=0,
        )
        cached = jnp.dot(
            queries, keys[k, :latent], preferred_element_type=jnp.float32
        ) + jnp.dot(turns, keys[k, latent:], preferred_element_type=jnp.float32)
        decoded = lax.dot_general(
            queries, newer[k, :, :latent], nt, preferred_element_type=jnp.float32
        ) + lax.dot_general(
            turns, newer[k, :, latent:], nt, preferred_element_type=jnp.float32
        )
        scores = jnp.concatenate([cached, decoded], axis=1)
        scores = jnp.where(token <= span * PAIR + within, scores * scale, -jnp.inf)
        spread = jnp.exp(scores - jnp.max(scores, axis=1, keepdims=True))
        weights = rounded(spread / jnp.sum(spread, axis=1, keepdims=True))
        mixed = rounded(
            lax.dot_general(
                weights[:, :capacity], keys[k, :latent], nt, preferred_element_type=jnp.float32
            )
            + jnp.dot(
                weights[:, capacity:], newer[k, :, :latent], preferred_element_type=jnp.float32
            )
        ).reshape(columns, PAIR * heads, latent)
        back_recv[u, 0] = mixed[0]
        for e in range(1, columns):
            back_send[u, e] = mixed[e]
        for e in downward:
            back_copy(u, e).start()
        return carry

    lax.fori_loop(0, spans * holders, unit, 0)
    wv_copy.wait()

    def project(span, members):
        held = len(members)
        for n, k in enumerate(members):
            u = span * holders + k
            for e in range(1, columns):
                back_copy(u, e).wait_recv()
            for e in range(columns):
                value = wide(back_recv[u, e])
                for c in range(cuts):
                    for s in range(PAIR):
                        at = (c * PAIR + s) * cut
                        for l in range(latent // LANES):
                            rows_mid[l, pl.ds(place(n, e, s) + c * cut, cut)] = value[
                                at : at + cut, lane(l)
                            ]

        def head(i, carry):
            at = pl.ds(i, held * columns * PAIR, stride=heads)
            picked = jnp.concatenate(
                [rounded(rows_mid[c, at]) for c in range(latent // LANES)], axis=1
            )
            rows_out[pl.ds(i, held * columns * PAIR, stride=heads)] = jnp.dot(
                picked, wv[i], preferred_element_type=jnp.float32
            )
            return carry

        lax.fori_loop(0, heads, head, 0, unroll=min(heads, 8))
        for n, k in enumerate(members):
            for e in range(columns):
                for s in range(PAIR):
                    value = rounded(rows_out[pl.ds(place(n, e, s), heads)])
                    if span and k < movers:
                        home[k, s, e] = value
                    else:
                        out_ref[span * PAIR + s, slot(e, k)] = value

    home_copies = [
        remote(home, home_recv.at[d - 1], home_ss.at[d - 1], home_rs.at[d - 1], at_group(d))
        for d in range(1, groups)
    ]
    project(0, list(range(holders)))
    project(1, list(range(movers)))
    for copy in home_copies:
        copy.start()
    if movers < holders:
        project(1, list(range(movers, holders)))
    for copy in home_copies:
        copy.wait()
    for k in range(movers):
        for e in range(columns):
            for s in range(PAIR):
                out_ref[PAIR + s, slot(e, k)] = rounded(
                    chosen(e, k, lambda n: home_recv[n, k, s, e])
                )

    def drain(u, carry):
        for e in range(1, columns):
            for c in range(cuts):
                lat_copy(u, e, c).wait_send()
            rot_copy(u, e).wait_send()
            back_copy(u, e).wait_send()
        return carry

    lax.fori_loop(0, spans * holders, drain, 0)


def local_part(heads):
    return max(heads // 4, 1)


def body(q_nope, q_rope, w_absorb_k, w_absorb_v, latent_cache, new_latent, lengths, moves):
    steps, slots, heads, width = q_nope.shape
    rope = q_rope.shape[3]
    latent = w_absorb_k.shape[2]
    holders, capacity, entries = latent_cache.shape
    movers = moves.shape[1]
    groups = lax.axis_size("grp")
    columns = lax.axis_size("head")
    scale = YARN_GAIN / math.sqrt(width + rope)
    assert steps == 2 * PAIR
    units = steps // PAIR * holders
    rows = (2 * holders - movers) * columns * PAIR * heads
    others = groups - 1
    bf16, f32 = jnp.bfloat16, jnp.float32
    dma = pltpu.SemaphoreType.DMA
    vmem = pl.BlockSpec(memory_space=pltpu.VMEM)
    smem = pl.BlockSpec(memory_space=pltpu.SMEM)
    hbm = pl.BlockSpec(memory_space=pl.ANY)
    parts = heads // local_part(heads)
    cuts = 1 if heads % 32 else 2
    return pl.pallas_call(
        functools.partial(kernel, groups, columns, scale),
        out_shape=jax.ShapeDtypeStruct(q_nope.shape, bf16),
        in_specs=[smem, smem, hbm, hbm, hbm, hbm, hbm, hbm],
        out_specs=vmem,
        scratch_shapes=[
            pltpu.VMEM(q_nope.shape, bf16),
            pltpu.VMEM(q_rope.shape, bf16),
            pltpu.VMEM(new_latent.shape, bf16),
            dma((3,)),
            pltpu.VMEM(w_absorb_k.shape, bf16),
            pltpu.VMEM(w_absorb_v.shape, bf16),
            pltpu.VMEM((holders, entries, capacity), bf16),
            pltpu.VMEM((holders, EXTRA, entries), bf16),
            dma((parts + holders + 1,)),
            pltpu.VMEM((rows, width), f32),
            pltpu.VMEM((latent // LANES, rows, LANES), f32),
            pltpu.VMEM((rows, width), f32),
            pltpu.VMEM((units, columns, cuts, PAIR * heads // cuts, latent), bf16),
            pltpu.VMEM((units, columns, cuts, PAIR * heads // cuts, latent), bf16),
            pltpu.VMEM((units, columns, heads, PAIR * rope), bf16),
            pltpu.VMEM((units, columns, heads, PAIR * rope), bf16),
            pltpu.VMEM((units, columns, PAIR * heads, latent), bf16),
            pltpu.VMEM((units, columns, PAIR * heads, latent), bf16),
            pltpu.VMEM((movers, PAIR + 1, columns, heads, width), bf16),
            pltpu.VMEM((others, movers, PAIR + 1, columns, heads, width), bf16),
            pltpu.VMEM((movers, 16, entries), bf16),
            pltpu.VMEM((others, movers, 16, entries), bf16),
            pltpu.VMEM((movers, PAIR, columns, heads, width), bf16),
            pltpu.VMEM((others, movers, PAIR, columns, heads, width), bf16),
            pltpu.VMEM((columns, movers, 8, LANES), jnp.int32),
            pltpu.VMEM((movers, 8, LANES), jnp.int32),
            dma((units, columns, cuts)), dma((units, columns, cuts)),
            dma((units, columns)), dma((units, columns)),
            dma((units, columns)), dma((units, columns)),
            dma((others,)), dma((others,)),
            dma((others,)), dma((others,)),
            dma((others,)), dma((others,)),
            dma((columns,)), dma((columns,)),
        ],
        compiler_params=pltpu.CompilerParams(
            collective_id=0, has_side_effects=True, vmem_limit_bytes=60 << 20
        ),
    )(lengths, moves, q_nope, q_rope, new_latent, w_absorb_k, w_absorb_v, jnp.swapaxes(latent_cache, 1, 2))


def solution(mesh):
    placed = (
        P(None, "grp", "head", None),
        P(None, "grp", "head", None),
        P("head", None, None),
        P("head", None, None),
        P(("grp", "head"), None, None),
        P(None, ("grp", "head"), None),
        P(),
        P("head", None),
    )
    return jax.shard_map(
        body, mesh=mesh, in_specs=placed, out_specs=P(None, "grp", "head", None), check_vma=False
    )
```

profile of v0, /device:TPU:0, one launch (start us, length us, event | category | flops | bytes accessed | tf_op | source)
XLA Modules:
  0.0 64.8 jit_solution(18040112571983525230)
XLA Ops:
  0.7 62.5 %shard_map.82 = bf16[4,8,32,128]{3,2,1,0:T(8,128)(2,1)} custom-call(s32[64]{0:T(128)} %length_ref.1, s32[1,1]{1,0:T(1,128)S(6)} %copy.10.move_ref, bf16[4,8,32,128]{3,2,1,0:T(8,128)(2,1)} %nope_hbm.1, bf16[4,8,32,64]{3,2,1,0:T(8,128)(2,1)} %rope_hbm.1, bf16[4,2,576]{2,1,0:T(2,128)(2,1)} %fresh_hbm.1, bf16[32,128,512]{2,1,0:T(8,128)(2,1)} %wk_hbm.1, ...), custom_call_target="tpu_custom_call" | custom-call | tf_op jit(solution)/shard_map/pallas_call | solution.py:411
  63.1 1.7 %copy.11 = bf16[4,8,32,128]{3,2,1,0:T(8,128)(2,1)} copy(bf16[4,8,32,128]{3,2,1,0:T(8,128)(2,1)} %shard_map.82) | data formatting | bytes 524288
where the time goes:
time: 65 us; the launch traced here: 64.8 us
  Pallas kernels  62.5 us (96%)
  local copies, waits for them, and re-layouts  1.67 us (3%)
  between operations  0.66 us (1%)
    pallas_call x1, Pallas kernels, body(): pl.pallas_call(functools.partial(kernel, groups, columns, scale), out_sha...  62.5 us
    unnamed x1, local copies, waits for them, and re-layouts  1.67 us

commit v1 on v0

v1 whole, which is shorter than its diff:
```python
import functools
import math

import jax
import jax.numpy as jnp
from jax import lax
from jax.experimental import pallas as pl
from jax.experimental.pallas import tpu as pltpu
from jax.sharding import PartitionSpec as P

PAIR = 2
EXTRA = 128
LANES = 128
YARN_GAIN = (0.1 * math.log(40.0) + 1.0) ** 2
MESH = pl.DeviceIdType.MESH


def lane(c):
    return slice(c * LANES, (c + 1) * LANES)


def rounded(value):
    return value.astype(jnp.bfloat16)


def wide(value):
    return value.astype(jnp.float32)


def kernel(
    groups, columns, scale,
    length_hbm, move_ref, nope_hbm, rope_hbm, fresh_hbm, wk_hbm, wv_hbm, cache_hbm,
    out_ref,
    length_ref, nope_ref, rope_ref, fresh_ref, entry_sem,
    wk, wv, keys, newer, local_sem,
    rows_in, rows_mid, rows_out,
    lat_send, lat_recv, rot_send, rot_recv, back_send, back_recv,
    mine, moved, mine_key, moved_key, home, home_recv, shift_of, shift_mine,
    lat_ss, lat_rs, rot_ss, rot_rs, back_ss, back_rs,
    mine_ss, mine_rs, key_ss, key_rs, home_ss, home_rs, shift_ss, shift_rs,
    plane_sem, open_sem,
):
    steps, _, heads, _ = nope_ref.shape
    holders, entries, capacity = cache_hbm.shape
    latent = wk.shape[2]
    rope = entries - latent
    movers = move_ref.shape[1]
    total = capacity + EXTRA
    cuts = lat_ss.shape[2]
    cut = heads // cuts
    rank = lax.axis_index("grp")
    column = lax.axis_index("head")
    parts = wk.shape[0] // local_part(heads)
    part = local_part(heads)
    hub = min(1, columns - 1)

    first = [(0, k) for k in range(holders)]
    rest = [(1, k) for k in range(movers, holders)]
    moving = [(1, k) for k in range(movers)]
    settled = first + rest
    number = {member: u for u, member in enumerate(settled + moving)}

    def at_column(e):
        return (rank, lax.rem(column + e + columns, columns))

    def at_group(d):
        return (lax.rem(rank + d + groups, groups), column)

    barrier = pltpu.get_barrier_semaphore()
    for e in range(1, columns):
        pl.semaphore_signal(barrier, inc=1, device_id=at_column(e), device_id_type=MESH)

    @pl.when(column == hub)
    def _():
        for d in range(1, groups):
            pl.semaphore_signal(barrier, inc=1, device_id=at_group(d), device_id_type=MESH)

    wk_copies = [
        pltpu.make_async_copy(
            wk_hbm.at[pl.ds(n * part, part)], wk.at[pl.ds(n * part, part)], local_sem.at[n]
        )
        for n in range(parts)
    ]
    key_copies = [
        pltpu.make_async_copy(
            cache_hbm.at[k], keys.at[k], local_sem.at[parts + k]
        )
        for k in range(holders)
    ]
    wv_copy = pltpu.make_async_copy(wv_hbm, wv, local_sem.at[parts + holders])
    entry_copies = [
        pltpu.make_async_copy(src, dst, entry_sem.at[n])
        for n, (src, dst) in enumerate(
            (
                (rope_hbm, rope_ref), (nope_hbm, nope_ref), (fresh_hbm, fresh_ref),
                (length_hbm, length_ref),
            )
        )
    ]
    for copy in entry_copies[:2] + wk_copies + entry_copies[2:]:
        copy.start()

    def remote(src, dst, send, recv, target):
        return pltpu.make_async_remote_copy(
            src_ref=src, dst_ref=dst, send_sem=send, recv_sem=recv,
            device_id=target, device_id_type=MESH,
        )

    sent = []

    def launch(copy):
        copy.start()
        sent.append(copy)

    def slot(e, k):
        return lax.rem(column + e, columns) * holders + k

    def turned(span, e, k):
        return jnp.concatenate(
            [rope_ref[span * PAIR + s, slot(e, k)] for s in range(PAIR)], axis=1
        )

    shift_copies = [
        remote(shift_mine, shift_of.at[e], shift_ss.at[e], shift_rs.at[e], at_column(-e))
        for e in range(1, columns)
    ]
    mine_copies = [
        remote(mine, moved.at[d - 1], mine_ss.at[d - 1], mine_rs.at[d - 1], at_group(-d))
        for d in range(1, groups)
    ]
    newer_copies = [
        remote(mine_key, moved_key.at[d - 1], key_ss.at[d - 1], key_rs.at[d - 1], at_group(-d))
        for d in range(1, groups)
    ]
    home_copies = [
        remote(home, home_recv.at[d - 1], home_ss.at[d - 1], home_rs.at[d - 1], at_group(d))
        for d in range(1, groups)
    ]

    per = PAIR * cut

    def lat_copy(member, e, c):
        u = number[member]
        at = pl.ds(c * per, per) if member == first[0] else pl.ds(0, PAIR * heads)
        return remote(
            lat_send.at[u, e, at], lat_recv.at[u, e, at], lat_ss.at[u, e, c], lat_rs.at[u, e, c],
            at_column(e),
        )

    def lat_pieces(member):
        return cuts if member == first[0] else 1

    def rot_copy(late, e):
        at = pl.ds(len(settled), len(moving)) if late else pl.ds(0, len(settled))
        return remote(
            rot_send.at[e, at], rot_recv.at[e, at], rot_ss.at[late, e], rot_rs.at[late, e],
            at_column(e),
        )

    def back_copy(member, e, c):
        u = number[member]
        at = pl.ds(c * per, per) if member in rest else pl.ds(0, PAIR * heads)
        return remote(
            back_send.at[u, e, at], back_recv.at[u, e, at], back_ss.at[u, e, c],
            back_rs.at[u, e, c], at_column(-e),
        )

    def back_pieces(member):
        return cuts if member in rest else 1

    low, high = jnp.int32(0), jnp.int32(columns - 1)
    upward, downward = [], []
    for _ in range(columns - 1):
        take_high = high - column >= column - low
        target = jnp.where(take_high, high, low)
        upward.append(lax.rem(target - column + columns, columns))
        downward.append(lax.rem(column - target + columns, columns))
        high = jnp.where(take_high, high - 1, high)
        low = jnp.where(take_high, low, low + 1)

    def chosen(e, k, options):
        found = wide(options(0))
        for d in range(2, groups):
            is_it = shift_of[e, k, 0:1, 0:1] == d
            found = jnp.where(is_it, wide(options(d - 1)), found)
        return found

    unit_rows = columns * PAIR * heads

    def place(m, e, s):
        return ((m * columns + e) * PAIR + s) * heads

    def turn(members, late):
        for span, k in members:
            u = number[span, k]
            for e in range(columns):
                if late:
                    pair = rounded(chosen(e, k, lambda n: moved[n, k, PAIR, e]))
                else:
                    pair = turned(span, e, k)
                if e:
                    rot_send[e, u] = pair
                else:
                    rot_recv[0, u] = pair

    def absorb(members, begin, late, between):
        count = len(members) * columns * PAIR
        for m, (span, k) in enumerate(members):
            for e in range(columns):
                for s in range(PAIR):
                    if late:
                        value = chosen(e, k, lambda n: moved[n, k, s, e])
                    else:
                        value = wide(nope_ref[span * PAIR + s, slot(e, k)])
                    rows_in[pl.ds(place(m, e, s), heads)] = value
        for n in range(parts):
            if not late:
                wk_copies[n].wait()

            def head(i, carry):
                picked = rounded(rows_in[pl.ds(i, count, stride=heads)])
                result = jnp.dot(picked, wk[i], preferred_element_type=jnp.float32)
                for c in range(latent // LANES):
                    rows_mid[c, pl.ds(i, count, stride=heads)] = result[:, lane(c)]
                return carry

            lax.fori_loop(n * part, (n + 1) * part, head, 0, unroll=True)
            if (n + 1) % (parts // cuts):
                continue
            c = n // (parts // cuts)
            for m, member in enumerate(members):
                u = number[member]
                for e in range(columns):
                    value = jnp.concatenate(
                        [
                            jnp.concatenate(
                                [
                                    rounded(rows_mid[l, pl.ds(place(m, e, s) + c * cut, cut)])
                                    for l in range(latent // LANES)
                                ],
                                axis=1,
                            )
                            for s in range(PAIR)
                        ],
                        axis=0,
                    )
                    if e:
                        lat_send[u, e, c * per : (c + 1) * per] = value
                    else:
                        lat_recv[u, 0, c * per : (c + 1) * per] = value
                if member in begin and (member == first[0] or c == cuts - 1):
                    for e in upward:
                        launch(lat_copy(member, e, c if lat_pieces(member) > 1 else 0))
            between(c)

    entry_copies[0].wait()
    turn(settled, 0)
    pl.semaphore_wait(
        barrier, jnp.where(column == hub, columns - 1 + groups - 1, columns - 1)
    )

    @pl.when(column == hub)
    def _():
        for d in range(1, groups):
            pl.semaphore_signal(plane_sem, inc=1, device_id=at_group(d), device_id_type=MESH)

    for e in upward:
        launch(rot_copy(0, e))
    for copy in entry_copies[1:]:
        copy.wait()
    row = lax.broadcasted_iota(jnp.int32, (16, entries), 0)

    def fresh_rows(k):
        found = jnp.zeros((16, entries), jnp.float32)
        for j in range(steps):
            found = jnp.where(row == j, wide(fresh_ref[j])[k : k + 1], found)
        return found

    def between(c):
        if c == 0:
            for k in range(movers):
                for e in range(columns):
                    for s in range(PAIR):
                        mine[k, s, e] = nope_ref[PAIR + s, slot(e, k)]
                    mine[k, PAIR, e] = turned(1, e, k)
                shift_mine[k] = jnp.full(shift_mine.shape[1:], move_ref[0, k], jnp.int32)
                shift_of[0, k] = jnp.full(shift_mine.shape[1:], move_ref[0, k], jnp.int32)
                mine_key[k] = rounded(fresh_rows(k))

            @pl.when(column == hub)
            def _():
                pl.semaphore_wait(plane_sem, groups - 1)
                for e in range(1, columns):
                    pl.semaphore_signal(
                        open_sem, inc=1, device_id=at_column(e), device_id_type=MESH
                    )

        if c == cuts - 1:
            @pl.when(column != hub)
            def _():
                pl.semaphore_wait(open_sem, 1)

            for copy in mine_copies + newer_copies + shift_copies:
                launch(copy)

    absorb(settled, first, 0, between)
    for copy in key_copies:
        copy.start()
    wv_copy.start()
    for k in range(holders):
        newer[k] = jnp.zeros((EXTRA, entries), jnp.bfloat16)
        newer[k, 0:16] = rounded(fresh_rows(k))
    for copy in key_copies:
        copy.wait()

    at_key = lax.broadcasted_iota(jnp.int32, (1, total), 1)
    at_row = lax.broadcasted_iota(jnp.int32, (unit_rows, 1), 0)
    within = lax.rem(lax.div(at_row, cut), PAIR)
    turns_in = set()

    def attend(member):
        span, k = member
        u = number[member]
        late = int(member in moving)
        for e in range(1, columns):
            for c in range(lat_pieces(member)):
                lat_copy(member, e, c).wait_recv()
            if late not in turns_in:
                rot_copy(late, e).wait_recv()
        turns_in.add(late)
        live = length_ref[(rank * columns + column) * holders + k]
        token = jnp.where(at_key < capacity, steps, at_key - capacity)
        token = jnp.where(at_key < live, -1, token)
        nt = (((1,), (1,)), ((), ()))
        queries = lat_recv[u].reshape(unit_rows, latent)
        turns = jnp.concatenate(
            [
                rot_recv[e, u][c * cut : (c + 1) * cut, s * rope : (s + 1) * rope]
                for e in range(columns)
                for c in range(cuts)
                for s in range(PAIR)
            ],
            axis=0,
        )
        cached = jnp.dot(
            queries, keys[k, :latent], preferred_element_type=jnp.float32
        ) + jnp.dot(turns, keys[k, latent:], preferred_element_type=jnp.float32)
        decoded = lax.dot_general(
            queries, newer[k, :, :latent], nt, preferred_element_type=jnp.float32
        ) + lax.dot_general(
            turns, newer[k, :, latent:], nt, preferred_element_type=jnp.float32
        )
        scores = jnp.concatenate([cached, decoded], axis=1)
        scores = jnp.where(token <= span * PAIR + within, scores * scale, -jnp.inf)
        spread = jnp.exp(scores - jnp.max(scores, axis=1, keepdims=True))
        weights = rounded(spread / jnp.sum(spread, axis=1, keepdims=True))
        mixed = rounded(
            lax.dot_general(
                weights[:, :capacity], keys[k, :latent], nt, preferred_element_type=jnp.float32
            )
            + jnp.dot(
                weights[:, capacity:], newer[k, :, :latent], preferred_element_type=jnp.float32
            )
        ).reshape(columns, PAIR * heads, latent)
        back_recv[u, 0] = mixed[0]
        for e in range(1, columns):
            back_send[u, e] = mixed[e]

    def give_back(members):
        for member in members:
            for c in range(back_pieces(member)):
                for e in downward:
                    launch(back_copy(member, e, c))

    def project(member, c):
        span, k = member
        u = number[member]
        chunks = range(cuts) if c is None else [c]
        for e in range(1, columns):
            for j in range(back_pieces(member)) if c is None else [c]:
                back_copy(member, e, j).wait_recv()
        for e in range(columns):
            for j in chunks:
                for s in range(PAIR):
                    at = (j * PAIR + s) * cut
                    value = wide(back_recv[u, e, at : at + cut])
                    for l in range(latent // LANES):
                        rows_mid[l, pl.ds(place(0, e, s) + j * cut, cut)] = value[:, lane(l)]

        def head(i, carry):
            at = pl.ds(i, columns * PAIR, stride=heads)
            picked = jnp.concatenate(
                [rounded(rows_mid[l, at]) for l in range(latent // LANES)], axis=1
            )
            rows_out[at] = jnp.dot(picked, wv[i], preferred_element_type=jnp.float32)
            return carry

        count = len(chunks) * cut
        start = chunks[0] * cut
        lax.fori_loop(start, start + count, head, 0, unroll=min(count, 8))
        for e in range(columns):
            for s in range(PAIR):
                value = rounded(rows_out[pl.ds(place(0, e, s) + start, count)])
                if member in moving:
                    home[k, s, e, start : start + count] = value
                else:
                    out_ref[span * PAIR + s, slot(e, k), start : start + count] = value

    attend(first[0])
    give_back(first[:1])
    for copy in mine_copies + newer_copies + shift_copies:
        copy.wait_recv()
    turn(moving, 1)
    for e in upward:
        launch(rot_copy(1, e))
    absorb(moving, moving, 1, lambda c: None)
    for member in rest:
        for e in upward:
            launch(lat_copy(member, e, 0))
    for member in first[1:]:
        attend(member)
    for k in range(movers):
        later = chosen(0, k, lambda n: moved_key[n, k])
        newer[k, 0:16] = rounded(jnp.where(row < PAIR, wide(newer[k, 0:16]), later))
    for member in moving:
        attend(member)
    give_back(moving + first[1:])
    wv_copy.wait()
    project(first[0], None)
    for member in rest:
        attend(member)
    give_back(rest)
    for member in moving:
        project(member, None)
    for copy in home_copies:
        launch(copy)
    for member in first[1:]:
        project(member, None)
    for copy in home_copies:
        copy.wait_recv()
    for k in range(movers):
        for e in range(columns):
            for s in range(PAIR):
                out_ref[PAIR + s, slot(e, k)] = rounded(
                    chosen(e, k, lambda n: home_recv[n, k, s, e])
                )
    for c in range(cuts):
        for member in rest:
            project(member, c)
    for copy in sent:
        copy.wait_send()


def local_part(heads):
    return max(heads // 4, 1)


def body(q_nope, q_rope, w_absorb_k, w_absorb_v, latent_cache, new_latent, lengths, moves):
    steps, slots, heads, width = q_nope.shape
    rope = q_rope.shape[3]
    latent = w_absorb_k.shape[2]
    holders, capacity, entries = latent_cache.shape
    movers = moves.shape[1]
    groups = lax.axis_size("grp")
    columns = lax.axis_size("head")
    scale = YARN_GAIN / math.sqrt(width + rope)
    assert steps == 2 * PAIR
    units = steps // PAIR * holders
    rows = (2 * holders - movers) * columns * PAIR * heads
    others = groups - 1
    bf16, f32 = jnp.bfloat16, jnp.float32
    dma = pltpu.SemaphoreType.DMA
    hbm = pl.BlockSpec(memory_space=pl.ANY)
    parts = heads // local_part(heads)
    cuts = 1 if heads % 32 else 2
    here = functools.partial(pltpu.with_memory_space_constraint, memory_space=pltpu.HBM)
    arrays = (
        q_nope, q_rope, new_latent, w_absorb_k, w_absorb_v, jnp.swapaxes(latent_cache, 1, 2)
    )
    return pl.pallas_call(
        functools.partial(kernel, groups, columns, scale),
        out_shape=pltpu.VMEM(q_nope.shape, bf16),
        in_specs=[hbm, pl.BlockSpec(memory_space=pltpu.SMEM)] + [hbm] * len(arrays),
        out_specs=pl.BlockSpec(memory_space=pltpu.VMEM),
        scratch_shapes=[
            pltpu.SMEM(lengths.shape, jnp.int32),
            pltpu.VMEM(q_nope.shape, bf16),
            pltpu.VMEM(q_rope.shape, bf16),
            pltpu.VMEM(new_latent.shape, bf16),
            dma((4,)),
            pltpu.VMEM(w_absorb_k.shape, bf16),
            pltpu.VMEM(w_absorb_v.shape, bf16),
            pltpu.VMEM((holders, entries, capacity), bf16),
            pltpu.VMEM((holders, EXTRA, entries), bf16),
            dma((parts + holders + 1,)),
            pltpu.VMEM((rows, width), f32),
            pltpu.VMEM((latent // LANES, rows, LANES), f32),
            pltpu.VMEM((rows, width), f32),
            pltpu.VMEM((units, columns, PAIR * heads, latent), bf16),
            pltpu.VMEM((units, columns, PAIR * heads, latent), bf16),
            pltpu.VMEM((columns, units, heads, PAIR * rope), bf16),
            pltpu.VMEM((columns, units, heads, PAIR * rope), bf16),
            pltpu.VMEM((units, columns, PAIR * heads, latent), bf16),
            pltpu.VMEM((units, columns, PAIR * heads, latent), bf16),
            pltpu.VMEM((movers, PAIR + 1, columns, heads, width), bf16),
            pltpu.VMEM((others, movers, PAIR + 1, columns, heads, width), bf16),
            pltpu.VMEM((movers, 16, entries), bf16),
            pltpu.VMEM((others, movers, 16, entries), bf16),
            pltpu.VMEM((movers, PAIR, columns, heads, width), bf16),
            pltpu.VMEM((others, movers, PAIR, columns, heads, width), bf16),
            pltpu.VMEM((columns, movers, 8, LANES), jnp.int32),
            pltpu.VMEM((movers, 8, LANES), jnp.int32),
            dma((units, columns, cuts)), dma((units, columns, cuts)),
            dma((2, columns)), dma((2, columns)),
            dma((units, columns, cuts)), dma((units, columns, cuts)),
            dma((others,)), dma((others,)),
            dma((others,)), dma((others,)),
            dma((others,)), dma((others,)),
            dma((columns,)), dma((columns,)),
            pltpu.SemaphoreType.REGULAR, pltpu.SemaphoreType.REGULAR,
        ],
        compiler_params=pltpu.CompilerParams(
            collective_id=0, has_side_effects=True, vmem_limit_bytes=44 << 20
        ),
    )(here(lengths), moves, *map(here, arrays))


def solution(mesh):
    placed = (
        P(None, "grp", "head", None),
        P(None, "grp", "head", None),
        P("head", None, None),
        P("head", None, None),
        P(("grp", "head"), None, None),
        P(None, ("grp", "head"), None),
        P(),
        P("head", None),
    )
    return jax.shard_map(
        body, mesh=mesh, in_specs=placed, out_specs=P(None, "grp", "head", None), check_vma=False
    )
```

time: 65 us -> 61.1 us (0.940)
  Pallas kernels: 62.5 us -> 59.1 us
  local copies, waits for them, and re-layouts: 1.67 us -> 0.71 us
    pallas_call x1, Pallas kernels: 62.5 us -> 59.1 us  [body(): pl.pallas_call(functools.partial(kernel, groups, columns, scale), out_sha...]
    unnamed x1, local copies, waits for them, and re-layouts: 1.67 us -> 0.71 us
where the time goes in v1:
time: 61.1 us; the launch traced here: 60.5 us
  Pallas kernels  59.1 us (97%)
  local copies, waits for them, and re-layouts  0.71 us (1%)
  between operations  0.66 us (1%)
    pallas_call x1, Pallas kernels, body(): pl.pallas_call(functools.partial(kernel, groups, columns, scale), out_sha...  59.1 us

profile of v1, /device:TPU:0, one launch (start us, length us, event | category | flops | bytes accessed | tf_op | source)
XLA Modules:
  0.0 60.5 jit_solution(1032767839721963540)
XLA Ops:
  0.7 59.1 %shard_map.82 = bf16[4,8,32,128]{3,2,1,0:T(8,128)(2,1)S(1)} custom-call(s32[64]{0:T(128)} %length_hbm.1, s32[1,1]{1,0:T(1,128)S(6)} %copy.11.move_ref, bf16[4,8,32,128]{3,2,1,0:T(8,128)(2,1)} %nope_hbm.1, bf16[4,8,32,64]{3,2,1,0:T(8,128)(2,1)} %rope_hbm.1, bf16[4,2,576]{2,1,0:T(2,128)(2,1)} %fresh_hbm.1, bf16[32,128,512]{2,1,0:T(8,128)(2,1)} %wk_hbm.1, ...), custom_call_target="tpu_custom_call" | custom-call | tf_op jit(solution)/shard_map/pallas_call | solution.py:480
  59.8 0.7 %copy.10 = bf16[4,8,32,128]{3,2,1,0:T(8,128)(2,1)} copy(bf16[4,8,32,128]{3,2,1,0:T(8,128)(2,1)S(1)} %shard_map.82) | data formatting | bytes 524288

commit v2 on v1

--- a/solution.py
+++ b/solution.py
@@ -38,7 +38,7 @@
     mine, moved, mine_key, moved_key, home, home_recv, shift_of, shift_mine,
     lat_ss, lat_rs, rot_ss, rot_rs, back_ss, back_rs,
     mine_ss, mine_rs, key_ss, key_rs, home_ss, home_rs, shift_ss, shift_rs,
-    plane_sem, open_sem,
+    near_sem, rank_sem, plane_sem, open_sem,
 ):
     steps, _, heads, _ = nope_ref.shape
     holders, entries, capacity = cache_hbm.shape
@@ -46,13 +46,12 @@
     rope = entries - latent
     movers = move_ref.shape[1]
     total = capacity + EXTRA
-    cuts = lat_ss.shape[2]
+    cuts = cuts_of(heads)
     cut = heads // cuts
     rank = lax.axis_index("grp")
     column = lax.axis_index("head")
     parts = wk.shape[0] // local_part(heads)
     part = local_part(heads)
-    hub = min(1, columns - 1)
 
     first = [(0, k) for k in range(holders)]
     rest = [(1, k) for k in range(movers, holders)]
@@ -68,11 +67,13 @@
 
     barrier = pltpu.get_barrier_semaphore()
     for e in range(1, columns):
-        pl.semaphore_signal(barrier, inc=1, device_id=at_column(e), device_id_type=MESH)
-
-    @pl.when(column == hub)
-    def _():
-        for d in range(1, groups):
+        @pl.when(column + e < columns)
+        def _():
+            pl.semaphore_signal(barrier, inc=1, device_id=at_column(e), device_id_type=MESH)
+
+    for d in range(1, groups):
+        @pl.when(jnp.logical_and(column == 0, rank + d < groups))
+        def _():
             pl.semaphore_signal(barrier, inc=1, device_id=at_group(d), device_id_type=MESH)
 
     wk_copies = [
@@ -81,13 +82,8 @@
         )
         for n in range(parts)
     ]
-    key_copies = [
-        pltpu.make_async_copy(
-            cache_hbm.at[k], keys.at[k], local_sem.at[parts + k]
-        )
-        for k in range(holders)
-    ]
-    wv_copy = pltpu.make_async_copy(wv_hbm, wv, local_sem.at[parts + holders])
+    key_copy = pltpu.make_async_copy(cache_hbm, keys, local_sem.at[parts])
+    wv_copy = pltpu.make_async_copy(wv_hbm, wv, local_sem.at[parts + 1])
     entry_copies = [
         pltpu.make_async_copy(src, dst, entry_sem.at[n])
         for n, (src, dst) in enumerate(
@@ -100,18 +96,32 @@
     for copy in entry_copies[:2] + wk_copies + entry_copies[2:]:
         copy.start()
 
+    below = jnp.where(column == 0, rank, column)
+
+    @pl.when(below > 0)
+    def _():
+        pl.semaphore_wait(barrier, below)
+
+    for e in range(1, columns):
+        @pl.when(column >= e)
+        def _():
+            pl.semaphore_signal(
+                near_sem.at[e - 1], inc=1, device_id=at_column(-e), device_id_type=MESH
+            )
+
+    for d in range(1, groups):
+        @pl.when(jnp.logical_and(column == 0, rank >= d))
+        def _():
+            pl.semaphore_signal(
+                rank_sem, inc=1, device_id=at_group(-d), device_id_type=MESH
+            )
+
     def remote(src, dst, send, recv, target):
         return pltpu.make_async_remote_copy(
             src_ref=src, dst_ref=dst, send_sem=send, recv_sem=recv,
             device_id=target, device_id_type=MESH,
         )
 
-    sent = []
-
-    def launch(copy):
-        copy.start()
-        sent.append(copy)
-
     def slot(e, k):
         return lax.rem(column + e, columns) * holders + k
 
@@ -120,53 +130,62 @@
             [rope_ref[span * PAIR + s, slot(e, k)] for s in range(PAIR)], axis=1
         )
 
-    shift_copies = [
-        remote(shift_mine, shift_of.at[e], shift_ss.at[e], shift_rs.at[e], at_column(-e))
-        for e in range(1, columns)
-    ]
-    mine_copies = [
-        remote(mine, moved.at[d - 1], mine_ss.at[d - 1], mine_rs.at[d - 1], at_group(-d))
-        for d in range(1, groups)
-    ]
-    newer_copies = [
-        remote(mine_key, moved_key.at[d - 1], key_ss.at[d - 1], key_rs.at[d - 1], at_group(-d))
-        for d in range(1, groups)
-    ]
-    home_copies = [
-        remote(home, home_recv.at[d - 1], home_ss.at[d - 1], home_rs.at[d - 1], at_group(d))
-        for d in range(1, groups)
-    ]
+    def shift_copy(e):
+        return remote(shift_mine, shift_of.at[columns - e], shift_ss, shift_rs, at_column(e))
+
+    def mine_copy(d):
+        return remote(mine, moved.at[d - 1], mine_ss, mine_rs, at_group(-d))
+
+    def newer_copy(d):
+        return remote(mine_key, moved_key.at[d - 1], key_ss, key_rs, at_group(-d))
+
+    def home_copy(d):
+        return remote(home, home_recv.at[d - 1], home_ss, home_rs, at_group(d))
 
     per = PAIR * cut
-
+    others = pl.ds(1, columns - 1)
     def lat_copy(member, e, c):
         u = number[member]
         at = pl.ds(c * per, per) if member == first[0] else pl.ds(0, PAIR * heads)
         return remote(
-            lat_send.at[u, e, at], lat_recv.at[u, e, at], lat_ss.at[u, e, c], lat_rs.at[u, e, c],
-            at_column(e),
-        )
-
-    def lat_pieces(member):
-        return cuts if member == first[0] else 1
+            lat_send.at[u, e, at], lat_recv.at[u, e, at], lat_ss, lat_rs.at[u], at_column(e)
+        )
+
+    def lat_all(member):
+        u = number[member]
+        return remote(
+            lat_send.at[u, others], lat_recv.at[u, others], lat_ss, lat_rs.at[u], at_column(1)
+        )
 
     def rot_copy(late, e):
         at = pl.ds(len(settled), len(moving)) if late else pl.ds(0, len(settled))
         return remote(
-            rot_send.at[e, at], rot_recv.at[e, at], rot_ss.at[late, e], rot_rs.at[late, e],
-            at_column(e),
-        )
+            rot_send.at[e, at], rot_recv.at[e, at], rot_ss, rot_rs.at[late], at_column(e)
+        )
+
+    def back_pieces(member):
+        return cuts if member in rest else 1
+
+    landed = {}
+    for member in settled + moving:
+        for c in range(back_pieces(member)):
+            landed[member, c] = len(landed)
 
     def back_copy(member, e, c):
         u = number[member]
         at = pl.ds(c * per, per) if member in rest else pl.ds(0, PAIR * heads)
         return remote(
-            back_send.at[u, e, at], back_recv.at[u, e, at], back_ss.at[u, e, c],
-            back_rs.at[u, e, c], at_column(-e),
-        )
-
-    def back_pieces(member):
-        return cuts if member in rest else 1
+            back_send.at[u, e, at], back_recv.at[u, e, at], back_ss,
+            back_rs.at[landed[member, c]], at_column(-e),
+        )
+
+    def back_all(member, c):
+        u = number[member]
+        at = pl.ds(c * per, per) if member in rest else pl.ds(0, PAIR * heads)
+        return remote(
+            back_send.at[u, others, at], back_recv.at[u, others, at], back_ss,
+            back_rs.at[landed[member, c]], at_column(1),
+        )
 
     low, high = jnp.int32(0), jnp.int32(columns - 1)
     upward, downward = [], []
@@ -177,6 +196,15 @@
         downward.append(lax.rem(column - target + columns, columns))
         high = jnp.where(take_high, high - 1, high)
         low = jnp.where(take_high, low, low + 1)
+
+    odd = lax.rem(rank, 2) == 1
+
+    def staggered(order):
+        turned_by_one = order[-1:] + order[:-1]
+        return [jnp.where(odd, b, a) for a, b in zip(order, turned_by_one)]
+
+    order_a = order_b = staggered(upward)
+    order_c = order_d = order_e = staggered(downward)
 
     def chosen(e, k, options):
         found = wide(options(0))
@@ -203,7 +231,7 @@
                 else:
                     rot_recv[0, u] = pair
 
-    def absorb(members, begin, late, between):
+    def absorb(members, late, after):
         count = len(members) * columns * PAIR
         for m, (span, k) in enumerate(members):
             for e in range(columns):
@@ -248,24 +276,19 @@
                         lat_send[u, e, c * per : (c + 1) * per] = value
                     else:
                         lat_recv[u, 0, c * per : (c + 1) * per] = value
-                if member in begin and (member == first[0] or c == cuts - 1):
-                    for e in upward:
-                        launch(lat_copy(member, e, c if lat_pieces(member) > 1 else 0))
-            between(c)
+            after(c)
 
     entry_copies[0].wait()
     turn(settled, 0)
-    pl.semaphore_wait(
-        barrier, jnp.where(column == hub, columns - 1 + groups - 1, columns - 1)
-    )
-
-    @pl.when(column == hub)
-    def _():
-        for d in range(1, groups):
-            pl.semaphore_signal(plane_sem, inc=1, device_id=at_group(d), device_id_type=MESH)
-
-    for e in upward:
-        launch(rot_copy(0, e))
+    for k in range(movers):
+        shift_mine[k] = jnp.full(shift_mine.shape[1:], move_ref[0, k], jnp.int32)
+        shift_of[0, k] = jnp.full(shift_mine.shape[1:], move_ref[0, k], jnp.int32)
+    for e in range(1, columns):
+        @pl.when(column + e >= columns)
+        def _():
+            rot_copy(0, e).start()
+            shift_copy(e).start()
+
     for copy in entry_copies[1:]:
         copy.wait()
     row = lax.broadcasted_iota(jnp.int32, (16, entries), 0)
@@ -276,18 +299,44 @@
             found = jnp.where(row == j, wide(fresh_ref[j])[k : k + 1], found)
         return found
 
-    def between(c):
+    def after_settled(c):
         if c == 0:
+            for e in range(1, columns):
+                @pl.when(column + e < columns)
+                def _():
+                    pl.semaphore_wait(near_sem.at[e - 1], 1)
+                    rot_copy(0, e).start()
+                    shift_copy(e).start()
+
+                lat_copy(first[0], e, 0).start()
+
+            @pl.when(jnp.logical_and(column == 0, rank < groups - 1))
+            def _():
+                pl.semaphore_wait(rank_sem, groups - 1 - rank)
+
+            @pl.when(column == 0)
+            def _():
+                for d in range(1, groups):
+                    pl.semaphore_signal(
+                        plane_sem, inc=1, device_id=at_group(d), device_id_type=MESH
+                    )
+
             for k in range(movers):
                 for e in range(columns):
                     for s in range(PAIR):
                         mine[k, s, e] = nope_ref[PAIR + s, slot(e, k)]
                     mine[k, PAIR, e] = turned(1, e, k)
-                shift_mine[k] = jnp.full(shift_mine.shape[1:], move_ref[0, k], jnp.int32)
-                shift_of[0, k] = jnp.full(shift_mine.shape[1:], move_ref[0, k], jnp.int32)
                 mine_key[k] = rounded(fresh_rows(k))
 
-            @pl.when(column == hub)
+        if c == cuts - 1:
+            if cuts > 1:
+                for e in order_a:
+                    lat_copy(first[0], e, c).start()
+            for member in first[1:]:
+                for e in order_a:
+                    lat_copy(member, e, 0).start()
+
+            @pl.when(column == 0)
             def _():
                 pl.semaphore_wait(plane_sem, groups - 1)
                 for e in range(1, columns):
@@ -295,23 +344,25 @@
                         open_sem, inc=1, device_id=at_column(e), device_id_type=MESH
                     )
 
-        if c == cuts - 1:
-            @pl.when(column != hub)
+            @pl.when(column > 0)
             def _():
                 pl.semaphore_wait(open_sem, 1)
 
-            for copy in mine_copies + newer_copies + shift_copies:
-                launch(copy)
-
-    absorb(settled, first, 0, between)
-    for copy in key_copies:
-        copy.start()
+            for d in range(1, groups):
+                mine_copy(d).start()
+            for d in range(1, groups):
+                newer_copy(d).start()
+            for member in rest:
+                for e in order_b:
+                    lat_copy(member, e, 0).start()
+
+    absorb(settled, 0, after_settled)
+    key_copy.start()
     wv_copy.start()
     for k in range(holders):
         newer[k] = jnp.zeros((EXTRA, entries), jnp.bfloat16)
         newer[k, 0:16] = rounded(fresh_rows(k))
-    for copy in key_copies:
-        copy.wait()
+    key_copy.wait()
 
     at_key = lax.broadcasted_iota(jnp.int32, (1, total), 1)
     at_row = lax.broadcasted_iota(jnp.int32, (unit_rows, 1), 0)
@@ -322,11 +373,13 @@
         span, k = member
         u = number[member]
         late = int(member in moving)
-        for e in range(1, columns):
-            for c in range(lat_pieces(member)):
-                lat_copy(member, e, c).wait_recv()
-            if late not in turns_in:
-                rot_copy(late, e).wait_recv()
+        lat_all(member).wait_recv()
+        if late not in turns_in:
+            at = pl.ds(len(settled), len(moving)) if late else pl.ds(0, len(settled))
+            remote(
+                rot_send.at[others, at], rot_recv.at[others, at], rot_ss, rot_rs.at[late],
+                at_column(1),
+            ).wait_recv()
         turns_in.add(late)
         live = length_ref[(rank * columns + column) * holders + k]
         token = jnp.where(at_key < capacity, steps, at_key - capacity)
@@ -366,19 +419,18 @@
         for e in range(1, columns):
             back_send[u, e] = mixed[e]
 
-    def give_back(members):
+    def give_back(members, order):
         for member in members:
             for c in range(back_pieces(member)):
-                for e in downward:
-                    launch(back_copy(member, e, c))
+                for e in order:
+                    back_copy(member, e, c).start()
 
     def project(member, c):
         span, k = member
         u = number[member]
         chunks = range(cuts) if c is None else [c]
-        for e in range(1, columns):
-            for j in range(back_pieces(member)) if c is None else [c]:
-                back_copy(member, e, j).wait_recv()
+        for j in range(back_pieces(member)) if c is None else [c]:
+            back_all(member, j).wait_recv()
         for e in range(columns):
             for j in chunks:
                 for s in range(PAIR):
@@ -407,37 +459,38 @@
                     out_ref[span * PAIR + s, slot(e, k), start : start + count] = value
 
     attend(first[0])
-    give_back(first[:1])
-    for copy in mine_copies + newer_copies + shift_copies:
+    shifts = remote(shift_of.at[others], shift_of.at[others], shift_ss, shift_rs, at_column(1))
+    mines = remote(moved, moved, mine_ss, mine_rs, at_group(1))
+    newers = remote(moved_key, moved_key, key_ss, key_rs, at_group(1))
+    homes = remote(home_recv, home_recv, home_ss, home_rs, at_group(1))
+    for copy in (shifts, mines, newers):
         copy.wait_recv()
     turn(moving, 1)
-    for e in upward:
-        launch(rot_copy(1, e))
-    absorb(moving, moving, 1, lambda c: None)
-    for member in rest:
-        for e in upward:
-            launch(lat_copy(member, e, 0))
-    for member in first[1:]:
+    for e in order_b:
+        rot_copy(1, e).start()
+    absorb(moving, 1, lambda c: None)
+    for member in moving:
+        for e in order_b:
+            lat_copy(member, e, 0).start()
+    give_back(first[:1], order_c)
+    for member in first[1:] + rest:
         attend(member)
     for k in range(movers):
         later = chosen(0, k, lambda n: moved_key[n, k])
         newer[k, 0:16] = rounded(jnp.where(row < PAIR, wide(newer[k, 0:16]), later))
     for member in moving:
         attend(member)
-    give_back(moving + first[1:])
+    give_back(moving + first[1:], order_d)
+    give_back(rest, order_e)
     wv_copy.wait()
     project(first[0], None)
-    for member in rest:
-        attend(member)
-    give_back(rest)
     for member in moving:
         project(member, None)
-    for copy in home_copies:
-        launch(copy)
+    for d in range(1, groups):
+        home_copy(d).start()
     for member in first[1:]:
         project(member, None)
-    for copy in home_copies:
-        copy.wait_recv()
+    homes.wait_recv()
     for k in range(movers):
         for e in range(columns):
             for s in range(PAIR):
@@ -447,12 +500,24 @@
     for c in range(cuts):
         for member in rest:
             project(member, c)
-    for copy in sent:
+    every = remote(lat_send.at[:, others], lat_recv.at[:, others], lat_ss, lat_rs.at[0], at_column(1))
+    every.wait_send()
+    remote(
+        rot_send.at[others], rot_recv.at[others], rot_ss, rot_rs.at[0], at_column(1)
+    ).wait_send()
+    remote(
+        back_send.at[:, others], back_recv.at[:, others], back_ss, back_rs.at[0], at_column(1)
+    ).wait_send()
+    for copy in (shifts, mines, newers, homes):
         copy.wait_send()
 
 
 def local_part(heads):
     return max(heads // 4, 1)
+
+
+def cuts_of(heads):
+    return 1 if heads % 32 else 2
 
 
 def body(q_nope, q_rope, w_absorb_k, w_absorb_v, latent_cache, new_latent, lengths, moves):
@@ -472,7 +537,7 @@
     dma = pltpu.SemaphoreType.DMA
     hbm = pl.BlockSpec(memory_space=pl.ANY)
     parts = heads // local_part(heads)
-    cuts = 1 if heads % 32 else 2
+    cuts = cuts_of(heads)
     here = functools.partial(pltpu.with_memory_space_constraint, memory_space=pltpu.HBM)
     arrays = (
         q_nope, q_rope, new_latent, w_absorb_k, w_absorb_v, jnp.swapaxes(latent_cache, 1, 2)
@@ -492,7 +557,7 @@
             pltpu.VMEM(w_absorb_v.shape, bf16),
             pltpu.VMEM((holders, entries, capacity), bf16),
             pltpu.VMEM((holders, EXTRA, entries), bf16),
-            dma((parts + holders + 1,)),
+            dma((parts + 2,)),
             pltpu.VMEM((rows, width), f32),
             pltpu.VMEM((latent // LANES, rows, LANES), f32),
             pltpu.VMEM((rows, width), f32),
@@ -510,13 +575,11 @@
             pltpu.VMEM((others, movers, PAIR, columns, heads, width), bf16),
             pltpu.VMEM((columns, movers, 8, LANES), jnp.int32),
             pltpu.VMEM((movers, 8, LANES), jnp.int32),
-            dma((units, columns, cuts)), dma((units, columns, cuts)),
-            dma((2, columns)), dma((2, columns)),
-            dma((units, columns, cuts)), dma((units, columns, cuts)),
-            dma((others,)), dma((others,)),
-            dma((others,)), dma((others,)),
-            dma((others,)), dma((others,)),
-            dma((columns,)), dma((columns,)),
+            dma, dma((units,)),
+            dma, dma((2,)),
+            dma, dma((units + (cuts - 1) * (holders - movers),)),
+            dma, dma, dma, dma, dma, dma, dma, dma,
+            pltpu.SemaphoreType.REGULAR((columns - 1,)), pltpu.SemaphoreType.REGULAR,
             pltpu.SemaphoreType.REGULAR, pltpu.SemaphoreType.REGULAR,
         ],
         compiler_params=pltpu.CompilerParams(

time: 61.1 us -> 57.6 us (0.943)
  Pallas kernels: 59.1 us -> 56.1 us
    pallas_call x1, Pallas kernels: 59.1 us -> 56.1 us  [body(): pl.pallas_call(functools.partial(kernel, groups, columns, scale), out_sha...]
where the time goes in v2:
time: 57.6 us; the launch traced here: 57.4 us
  Pallas kernels  56.1 us (97%)
  local copies, waits for them, and re-layouts  0.71 us (1%)
  between operations  0.66 us (1%)
    pallas_call x1, Pallas kernels, body(): pl.pallas_call(functools.partial(kernel, groups, columns, scale), out_sha...  56.1 us

profile of v2, /device:TPU:0, one launch (start us, length us, event | category | flops | bytes accessed | tf_op | source)
XLA Modules:
  0.0 57.4 jit_solution(15675443508241481960)
XLA Ops:
  0.7 56.1 %shard_map.82 = bf16[4,8,32,128]{3,2,1,0:T(8,128)(2,1)S(1)} custom-call(s32[64]{0:T(128)} %length_hbm.1, s32[1,1]{1,0:T(1,128)S(6)} %copy.11.move_ref, bf16[4,8,32,128]{3,2,1,0:T(8,128)(2,1)} %nope_hbm.1, bf16[4,8,32,64]{3,2,1,0:T(8,128)(2,1)} %rope_hbm.1, bf16[4,2,576]{2,1,0:T(2,128)(2,1)} %fresh_hbm.1, bf16[32,128,512]{2,1,0:T(8,128)(2,1)} %wk_hbm.1, ...), custom_call_target="tpu_custom_call" | custom-call | tf_op jit(solution)/shard_map/pallas_call | solution.py:545
  56.7 0.7 %copy.10 = bf16[4,8,32,128]{3,2,1,0:T(8,128)(2,1)} copy(bf16[4,8,32,128]{3,2,1,0:T(8,128)(2,1)S(1)} %shard_map.82) | data formatting | bytes 524288

commit v3 on v2

--- a/solution.py
+++ b/solution.py
@@ -34,11 +34,11 @@
     length_ref, nope_ref, rope_ref, fresh_ref, entry_sem,
     wk, wv, keys, newer, local_sem,
     rows_in, rows_mid, rows_out,
-    lat_send, lat_recv, rot_send, rot_recv, back_send, back_recv,
+    lat_send, lat_recv, late_send, late_recv, rot_send, rot_recv, back_send, back_recv,
     mine, moved, mine_key, moved_key, home, home_recv, shift_of, shift_mine,
-    lat_ss, lat_rs, rot_ss, rot_rs, back_ss, back_rs,
+    lat_ss, lat_rs, late_ss, late_rs, rot_ss, rot_rs, back_ss, back_rs,
     mine_ss, mine_rs, key_ss, key_rs, home_ss, home_rs, shift_ss, shift_rs,
-    near_sem, rank_sem, plane_sem, open_sem,
+    near_sem, rank_sem,
 ):
     steps, _, heads, _ = nope_ref.shape
     holders, entries, capacity = cache_hbm.shape
@@ -72,7 +72,7 @@
             pl.semaphore_signal(barrier, inc=1, device_id=at_column(e), device_id_type=MESH)
 
     for d in range(1, groups):
-        @pl.when(jnp.logical_and(column == 0, rank + d < groups))
+        @pl.when(rank + d < groups)
         def _():
             pl.semaphore_signal(barrier, inc=1, device_id=at_group(d), device_id_type=MESH)
 
@@ -93,10 +93,10 @@
             )
         )
     ]
-    for copy in entry_copies[:2] + wk_copies + entry_copies[2:]:
+    for copy in entry_copies[:2] + wk_copies[:1]:
         copy.start()
 
-    below = jnp.where(column == 0, rank, column)
+    below = rank + column
 
     @pl.when(below > 0)
     def _():
@@ -110,7 +110,7 @@
             )
 
     for d in range(1, groups):
-        @pl.when(jnp.logical_and(column == 0, rank >= d))
+        @pl.when(rank >= d)
         def _():
             pl.semaphore_signal(
                 rank_sem, inc=1, device_id=at_group(-d), device_id_type=MESH
@@ -144,18 +144,23 @@
 
     per = PAIR * cut
     others = pl.ds(1, columns - 1)
-    def lat_copy(member, e, c):
-        u = number[member]
-        at = pl.ds(c * per, per) if member == first[0] else pl.ds(0, PAIR * heads)
-        return remote(
-            lat_send.at[u, e, at], lat_recv.at[u, e, at], lat_ss, lat_rs.at[u], at_column(e)
-        )
-
-    def lat_all(member):
-        u = number[member]
-        return remote(
-            lat_send.at[u, others], lat_recv.at[u, others], lat_ss, lat_rs.at[u], at_column(1)
-        )
+    halves = [(0, cuts // 2), (cuts // 2, cuts)] if cuts > 1 else [(0, 1)]
+    back_pieces = {member: [(0, cuts)] for member in number}
+    if cuts > 1:
+        for member in rest:
+            back_pieces[member] = halves
+
+    def rows_of(piece):
+        return pl.ds(piece[0] * per, (piece[1] - piece[0]) * per)
+
+    def lat_copy(e, c):
+        return remote(lat_send.at[e, c], lat_recv.at[e, c], lat_ss, lat_rs, at_column(e))
+
+    def late_copy(e):
+        return remote(late_send.at[e], late_recv.at[e], late_ss, late_rs, at_column(e))
+
+    lats = remote(lat_send.at[others], lat_recv.at[others], lat_ss, lat_rs, at_column(1))
+    lates = remote(late_send.at[others], late_recv.at[others], late_ss, late_rs, at_column(1))
 
     def rot_copy(late, e):
         at = pl.ds(len(settled), len(moving)) if late else pl.ds(0, len(settled))
@@ -163,17 +168,14 @@
             rot_send.at[e, at], rot_recv.at[e, at], rot_ss, rot_rs.at[late], at_column(e)
         )
 
-    def back_pieces(member):
-        return cuts if member in rest else 1
-
     landed = {}
     for member in settled + moving:
-        for c in range(back_pieces(member)):
+        for c in range(len(back_pieces[member])):
             landed[member, c] = len(landed)
 
     def back_copy(member, e, c):
         u = number[member]
-        at = pl.ds(c * per, per) if member in rest else pl.ds(0, PAIR * heads)
+        at = rows_of(back_pieces[member][c])
         return remote(
             back_send.at[u, e, at], back_recv.at[u, e, at], back_ss,
             back_rs.at[landed[member, c]], at_column(-e),
@@ -181,30 +183,33 @@
 
     def back_all(member, c):
         u = number[member]
-        at = pl.ds(c * per, per) if member in rest else pl.ds(0, PAIR * heads)
+        at = rows_of(back_pieces[member][c])
         return remote(
             back_send.at[u, others, at], back_recv.at[u, others, at], back_ss,
             back_rs.at[landed[member, c]], at_column(1),
         )
 
     low, high = jnp.int32(0), jnp.int32(columns - 1)
-    upward, downward = [], []
+    near = []
     for _ in range(columns - 1):
-        take_high = high - column >= column - low
-        target = jnp.where(take_high, high, low)
-        upward.append(lax.rem(target - column + columns, columns))
-        downward.append(lax.rem(column - target + columns, columns))
+        above, below = high - column, column - low
+        take_high = jnp.where(2 * column < columns, above >= below, above > below)
+        near.insert(0, jnp.where(take_high, high, low))
         high = jnp.where(take_high, high - 1, high)
         low = jnp.where(take_high, low, low + 1)
-
-    odd = lax.rem(rank, 2) == 1
-
-    def staggered(order):
-        turned_by_one = order[-1:] + order[:-1]
-        return [jnp.where(odd, b, a) for a, b in zip(order, turned_by_one)]
-
-    order_a = order_b = staggered(upward)
-    order_c = order_d = order_e = staggered(downward)
+    near_up = [lax.rem(target - column + columns, columns) for target in near]
+    near_down = [lax.rem(column - target + columns, columns) for target in near]
+
+    far_down = near_down[::-1]
+    end = jnp.logical_or(column == 0, column == columns - 1)
+
+    def send_back(pieces, order):
+        for member, c in pieces:
+            for e in order:
+                back_copy(member, e, c).start()
+
+    def pieces_of(members, table):
+        return [(member, c) for member in members for c in range(len(table[member]))]
 
     def chosen(e, k, options):
         found = wide(options(0))
@@ -259,26 +264,31 @@
             for m, member in enumerate(members):
                 u = number[member]
                 for e in range(columns):
-                    value = jnp.concatenate(
-                        [
-                            jnp.concatenate(
-                                [
-                                    rounded(rows_mid[l, pl.ds(place(m, e, s) + c * cut, cut)])
-                                    for l in range(latent // LANES)
-                                ],
-                                axis=1,
-                            )
-                            for s in range(PAIR)
-                        ],
-                        axis=0,
+                    value = rounded(
+                        jnp.concatenate(
+                            [
+                                jnp.concatenate(
+                                    [
+                                        rows_mid[l, pl.ds(place(m, e, s) + c * cut, cut)]
+                                        for l in range(latent // LANES)
+                                    ],
+                                    axis=1,
+                                )
+                                for s in range(PAIR)
+                            ],
+                            axis=0,
+                        )
                     )
-                    if e:
-                        lat_send[u, e, c * per : (c + 1) * per] = value
+                    if late:
+                        to, at = (late_send if e else late_recv), (e, m, c)
                     else:
-                        lat_recv[u, 0, c * per : (c + 1) * per] = value
+                        to, at = (lat_send if e else lat_recv), (e, c, m)
+                    to[at] = value
             after(c)
 
     entry_copies[0].wait()
+    for copy in wk_copies[1:] + entry_copies[2:]:
+        copy.start()
     turn(settled, 0)
     for k in range(movers):
         shift_mine[k] = jnp.full(shift_mine.shape[1:], move_ref[0, k], jnp.int32)
@@ -289,8 +299,7 @@
             rot_copy(0, e).start()
             shift_copy(e).start()
 
-    for copy in entry_copies[1:]:
-        copy.wait()
+    entry_copies[1].wait()
     row = lax.broadcasted_iota(jnp.int32, (16, entries), 0)
 
     def fresh_rows(k):
@@ -300,27 +309,29 @@
         return found
 
     def after_settled(c):
-        if c == 0:
-            for e in range(1, columns):
+        asked = 0
+        for e in range(1, columns):
+            @pl.when(column + e >= columns)
+            def _():
+                lat_copy(e, c).start()
+
+            if c == asked:
                 @pl.when(column + e < columns)
                 def _():
                     pl.semaphore_wait(near_sem.at[e - 1], 1)
                     rot_copy(0, e).start()
                     shift_copy(e).start()
 
-                lat_copy(first[0], e, 0).start()
-
-            @pl.when(jnp.logical_and(column == 0, rank < groups - 1))
-            def _():
-                pl.semaphore_wait(rank_sem, groups - 1 - rank)
-
-            @pl.when(column == 0)
-            def _():
-                for d in range(1, groups):
-                    pl.semaphore_signal(
-                        plane_sem, inc=1, device_id=at_group(d), device_id_type=MESH
-                    )
-
+        if c >= asked:
+            for e in range(1, columns):
+                @pl.when(column + e < columns)
+                def _():
+                    for j in range(c + 1) if c == asked else [c]:
+                        lat_copy(e, j).start()
+
+        if c == 0:
+            for copy in entry_copies[2:]:
+                copy.wait()
             for k in range(movers):
                 for e in range(columns):
                     for s in range(PAIR):
@@ -329,32 +340,14 @@
                 mine_key[k] = rounded(fresh_rows(k))
 
         if c == cuts - 1:
-            if cuts > 1:
-                for e in order_a:
-                    lat_copy(first[0], e, c).start()
-            for member in first[1:]:
-                for e in order_a:
-                    lat_copy(member, e, 0).start()
-
-            @pl.when(column == 0)
+            @pl.when(rank < groups - 1)
             def _():
-                pl.semaphore_wait(plane_sem, groups - 1)
-                for e in range(1, columns):
-                    pl.semaphore_signal(
-                        open_sem, inc=1, device_id=at_column(e), device_id_type=MESH
-                    )
-
-            @pl.when(column > 0)
-            def _():
-                pl.semaphore_wait(open_sem, 1)
+                pl.semaphore_wait(rank_sem, groups - 1 - rank)
 
             for d in range(1, groups):
                 mine_copy(d).start()
             for d in range(1, groups):
                 newer_copy(d).start()
-            for member in rest:
-                for e in order_b:
-                    lat_copy(member, e, 0).start()
 
     absorb(settled, 0, after_settled)
     key_copy.start()
@@ -373,7 +366,8 @@
         span, k = member
         u = number[member]
         late = int(member in moving)
-        lat_all(member).wait_recv()
+        if late not in turns_in:
+            (lates if late else lats).wait_recv()
         if late not in turns_in:
             at = pl.ds(len(settled), len(moving)) if late else pl.ds(0, len(settled))
             remote(
@@ -385,15 +379,20 @@
         token = jnp.where(at_key < capacity, steps, at_key - capacity)
         token = jnp.where(at_key < live, -1, token)
         nt = (((1,), (1,)), ((), ()))
-        queries = lat_recv[u].reshape(unit_rows, latent)
-        turns = jnp.concatenate(
-            [
-                rot_recv[e, u][c * cut : (c + 1) * cut, s * rope : (s + 1) * rope]
-                for e in range(columns)
-                for c in range(cuts)
-                for s in range(PAIR)
-            ],
-            axis=0,
+        queries = (late_recv[:, u - len(settled)] if late else lat_recv[:, :, u]).reshape(
+            unit_rows, latent
+        )
+        pairs = [wide(rot_recv[e, u]) for e in range(columns)]
+        turns = rounded(
+            jnp.concatenate(
+                [
+                    pairs[e][c * cut : (c + 1) * cut, s * rope : (s + 1) * rope]
+                    for e in range(columns)
+                    for c in range(cuts)
+                    for s in range(PAIR)
+                ],
+                axis=0,
+            )
         )
         cached = jnp.dot(
             queries, keys[k, :latent], preferred_element_type=jnp.float32
@@ -419,25 +418,20 @@
         for e in range(1, columns):
             back_send[u, e] = mixed[e]
 
-    def give_back(members, order):
-        for member in members:
-            for c in range(back_pieces(member)):
-                for e in order:
-                    back_copy(member, e, c).start()
-
     def project(member, c):
         span, k = member
         u = number[member]
-        chunks = range(cuts) if c is None else [c]
-        for j in range(back_pieces(member)) if c is None else [c]:
+        low, high = back_pieces[member][c] if c is not None else (0, cuts)
+        for j in range(len(back_pieces[member])) if c is None else [c]:
             back_all(member, j).wait_recv()
         for e in range(columns):
-            for j in chunks:
+            for j in range(low, high):
+                value = wide(back_recv[u, e, j * per : (j + 1) * per])
                 for s in range(PAIR):
-                    at = (j * PAIR + s) * cut
-                    value = wide(back_recv[u, e, at : at + cut])
                     for l in range(latent // LANES):
-                        rows_mid[l, pl.ds(place(0, e, s) + j * cut, cut)] = value[:, lane(l)]
+                        rows_mid[l, pl.ds(place(0, e, s) + j * cut, cut)] = value[
+                            s * cut : (s + 1) * cut, lane(l)
+                        ]
 
         def head(i, carry):
             at = pl.ds(i, columns * PAIR, stride=heads)
@@ -447,8 +441,8 @@
             rows_out[at] = jnp.dot(picked, wv[i], preferred_element_type=jnp.float32)
             return carry
 
-        count = len(chunks) * cut
-        start = chunks[0] * cut
+        count = (high - low) * cut
+        start = low * cut
         lax.fori_loop(start, start + count, head, 0, unroll=min(count, 8))
         for e in range(columns):
             for s in range(PAIR):
@@ -458,38 +452,52 @@
                 else:
                     out_ref[span * PAIR + s, slot(e, k), start : start + count] = value
 
-    attend(first[0])
     shifts = remote(shift_of.at[others], shift_of.at[others], shift_ss, shift_rs, at_column(1))
     mines = remote(moved, moved, mine_ss, mine_rs, at_group(1))
     newers = remote(moved_key, moved_key, key_ss, key_rs, at_group(1))
     homes = remote(home_recv, home_recv, home_ss, home_rs, at_group(1))
-    for copy in (shifts, mines, newers):
+    for copy in (shifts, mines):
         copy.wait_recv()
     turn(moving, 1)
-    for e in order_b:
+    for e in near_up:
         rot_copy(1, e).start()
     absorb(moving, 1, lambda c: None)
-    for member in moving:
-        for e in order_b:
-            lat_copy(member, e, 0).start()
-    give_back(first[:1], order_c)
-    for member in first[1:] + rest:
+    for e in near_up:
+        late_copy(e).start()
+    attend(first[0])
+
+    @pl.when(jnp.logical_not(end))
+    def _():
+        send_back(pieces_of(first[:1], back_pieces), far_down)
+
+    for member in settled[1:]:
         attend(member)
+    newers.wait_recv()
     for k in range(movers):
         later = chosen(0, k, lambda n: moved_key[n, k])
         newer[k, 0:16] = rounded(jnp.where(row < PAIR, wide(newer[k, 0:16]), later))
     for member in moving:
         attend(member)
-    give_back(moving + first[1:], order_d)
-    give_back(rest, order_e)
+    send_back(pieces_of(moving, back_pieces), far_down)
+
+    @pl.when(end)
+    def _():
+        send_back(pieces_of(first[:1], back_pieces), far_down)
+
+    send_back(pieces_of(settled[1:], back_pieces), near_down[:1])
+    send_back(pieces_of(first[1:], back_pieces), far_down[:-1])
+    for e in far_down[:-1]:
+        send_back(pieces_of(rest, back_pieces), [e])
     wv_copy.wait()
-    project(first[0], None)
     for member in moving:
         project(member, None)
     for d in range(1, groups):
         home_copy(d).start()
-    for member in first[1:]:
+    for member in first:
         project(member, None)
+    for c in range(len(halves)):
+        for member in rest:
+            project(member, c)
     homes.wait_recv()
     for k in range(movers):
         for e in range(columns):
@@ -497,18 +505,13 @@
                 out_ref[PAIR + s, slot(e, k)] = rounded(
                     chosen(e, k, lambda n: home_recv[n, k, s, e])
                 )
-    for c in range(cuts):
-        for member in rest:
-            project(member, c)
-    every = remote(lat_send.at[:, others], lat_recv.at[:, others], lat_ss, lat_rs.at[0], at_column(1))
-    every.wait_send()
     remote(
         rot_send.at[others], rot_recv.at[others], rot_ss, rot_rs.at[0], at_column(1)
     ).wait_send()
     remote(
         back_send.at[:, others], back_recv.at[:, others], back_ss, back_rs.at[0], at_column(1)
     ).wait_send()
-    for copy in (shifts, mines, newers, homes):
+    for copy in (lats, lates, shifts, mines, newers, homes):
         copy.wait_send()
 
 
@@ -517,7 +520,7 @@
 
 
 def cuts_of(heads):
-    return 1 if heads % 32 else 2
+    return 1 if heads % 32 else 4
 
 
 def body(q_nope, q_rope, w_absorb_k, w_absorb_v, latent_cache, new_latent, lengths, moves):
@@ -561,8 +564,10 @@
             pltpu.VMEM((rows, width), f32),
             pltpu.VMEM((latent // LANES, rows, LANES), f32),
             pltpu.VMEM((rows, width), f32),
-            pltpu.VMEM((units, columns, PAIR * heads, latent), bf16),
-            pltpu.VMEM((units, columns, PAIR * heads, latent), bf16),
+            pltpu.VMEM((columns, cuts, units - movers, PAIR * heads // cuts, latent), bf16),
+            pltpu.VMEM((columns, cuts, units - movers, PAIR * heads // cuts, latent), bf16),
+            pltpu.VMEM((columns, movers, cuts, PAIR * heads // cuts, latent), bf16),
+            pltpu.VMEM((columns, movers, cuts, PAIR * heads // cuts, latent), bf16),
             pltpu.VMEM((columns, units, heads, PAIR * rope), bf16),
             pltpu.VMEM((columns, units, heads, PAIR * rope), bf16),
             pltpu.VMEM((units, columns, PAIR * heads, latent), bf16),
@@ -575,12 +580,11 @@
             pltpu.VMEM((others, movers, PAIR, columns, heads, width), bf16),
             pltpu.VMEM((columns, movers, 8, LANES), jnp.int32),
             pltpu.VMEM((movers, 8, LANES), jnp.int32),
-            dma, dma((units,)),
+            dma, dma, dma, dma,
             dma, dma((2,)),
-            dma, dma((units + (cuts - 1) * (holders - movers),)),
+            dma, dma((2 * units,)),
             dma, dma, dma, dma, dma, dma, dma, dma,
             pltpu.SemaphoreType.REGULAR((columns - 1,)), pltpu.SemaphoreType.REGULAR,
-            pltpu.SemaphoreType.REGULAR, pltpu.SemaphoreType.REGULAR,
         ],
         compiler_params=pltpu.CompilerParams(
             collective_id=0, has_side_effects=True, vmem_limit_bytes=44 << 20

time: 57.6 us -> 57.1 us (level)
  no operation moved by 1% of the time
where the time goes in v3:
time: 57.1 us; the launch traced here: 57 us
  Pallas kernels  55.6 us (97%)
  local copies, waits for them, and re-layouts  0.71 us (1%)
  between operations  0.66 us (1%)
    pallas_call x1, Pallas kernels, body(): pl.pallas_call(functools.partial(kernel, groups, columns, scale), out_sha...  55.6 us

profile of v3, /device:TPU:0, one launch (start us, length us, event | category | flops | bytes accessed | tf_op | source)
XLA Modules:
  0.0 57.0 jit_solution(809229546182389876)
XLA Ops:
  0.7 55.6 %shard_map.82 = bf16[4,8,32,128]{3,2,1,0:T(8,128)(2,1)S(1)} custom-call(s32[64]{0:T(128)} %length_hbm.1, s32[1,1]{1,0:T(1,128)S(6)} %copy.11.move_ref, bf16[4,8,32,128]{3,2,1,0:T(8,128)(2,1)} %nope_hbm.1, bf16[4,8,32,64]{3,2,1,0:T(8,128)(2,1)} %rope_hbm.1, bf16[4,2,576]{2,1,0:T(2,128)(2,1)} %fresh_hbm.1, bf16[32,128,512]{2,1,0:T(8,128)(2,1)} %wk_hbm.1, ...), custom_call_target="tpu_custom_call" | custom-call | tf_op jit(solution)/shard_map/pallas_call | solution.py:548
  56.3 0.7 %copy.10 = bf16[4,8,32,128]{3,2,1,0:T(8,128)(2,1)} copy(bf16[4,8,32,128]{3,2,1,0:T(8,128)(2,1)S(1)} %shard_map.82) | data formatting | bytes 524288

commit v4 on v3

--- a/solution.py
+++ b/solution.py
@@ -144,7 +144,7 @@
 
     per = PAIR * cut
     others = pl.ds(1, columns - 1)
-    halves = [(0, cuts // 2), (cuts // 2, cuts)] if cuts > 1 else [(0, 1)]
+    halves = [(0, cuts - 1), (cuts - 1, cuts)] if cuts > 1 else [(0, 1)]
     back_pieces = {member: [(0, cuts)] for member in number}
     if cuts > 1:
         for member in rest:
@@ -470,8 +470,6 @@
     def _():
         send_back(pieces_of(first[:1], back_pieces), far_down)
 
-    for member in settled[1:]:
-        attend(member)
     newers.wait_recv()
     for k in range(movers):
         later = chosen(0, k, lambda n: moved_key[n, k])
@@ -484,6 +482,8 @@
     def _():
         send_back(pieces_of(first[:1], back_pieces), far_down)
 
+    for member in settled[1:]:
+        attend(member)
     send_back(pieces_of(settled[1:], back_pieces), near_down[:1])
     send_back(pieces_of(first[1:], back_pieces), far_down[:-1])
     for e in far_down[:-1]:

time: 57.1 us -> 56 us (0.981)
  Pallas kernels: 55.6 us -> 54.4 us
    pallas_call x1, Pallas kernels: 55.6 us -> 54.4 us  [body(): pl.pallas_call(functools.partial(kernel, groups, columns, scale), out_sha...]
where the time goes in v4:
time: 56 us; the launch traced here: 55.8 us
  Pallas kernels  54.4 us (97%)
  local copies, waits for them, and re-layouts  0.71 us (1%)
  between operations  0.66 us (1%)
    pallas_call x1, Pallas kernels, body(): pl.pallas_call(functools.partial(kernel, groups, columns, scale), out_sha...  54.4 us

profile of v4, /device:TPU:0, one launch (start us, length us, event | category | flops | bytes accessed | tf_op | source)
XLA Modules:
  0.0 55.8 jit_solution(10741567224794241557)
XLA Ops:
  0.7 54.4 %shard_map.82 = bf16[4,8,32,128]{3,2,1,0:T(8,128)(2,1)S(1)} custom-call(s32[64]{0:T(128)} %length_hbm.1, s32[1,1]{1,0:T(1,128)S(6)} %copy.11.move_ref, bf16[4,8,32,128]{3,2,1,0:T(8,128)(2,1)} %nope_hbm.1, bf16[4,8,32,64]{3,2,1,0:T(8,128)(2,1)} %rope_hbm.1, bf16[4,2,576]{2,1,0:T(2,128)(2,1)} %fresh_hbm.1, bf16[32,128,512]{2,1,0:T(8,128)(2,1)} %wk_hbm.1, ...), custom_call_target="tpu_custom_call" | custom-call | tf_op jit(solution)/shard_map/pallas_call | solution.py:548
  55.0 0.7 %copy.10 = bf16[4,8,32,128]{3,2,1,0:T(8,128)(2,1)} copy(bf16[4,8,32,128]{3,2,1,0:T(8,128)(2,1)S(1)} %shard_map.82) | data formatting | bytes 524288

commit v5 on v4

--- a/solution.py
+++ b/solution.py
@@ -38,7 +38,7 @@
     mine, moved, mine_key, moved_key, home, home_recv, shift_of, shift_mine,
     lat_ss, lat_rs, late_ss, late_rs, rot_ss, rot_rs, back_ss, back_rs,
     mine_ss, mine_rs, key_ss, key_rs, home_ss, home_rs, shift_ss, shift_rs,
-    near_sem, rank_sem,
+    near_sem, rank_sem, open_sem,
 ):
     steps, _, heads, _ = nope_ref.shape
     holders, entries, capacity = cache_hbm.shape
@@ -71,9 +71,9 @@
         def _():
             pl.semaphore_signal(barrier, inc=1, device_id=at_column(e), device_id_type=MESH)
 
-    for d in range(1, groups):
-        @pl.when(rank + d < groups)
-        def _():
+    @pl.when(rank == 0)
+    def _():
+        for d in range(1, groups):
             pl.semaphore_signal(barrier, inc=1, device_id=at_group(d), device_id_type=MESH)
 
     wk_copies = [
@@ -96,7 +96,7 @@
     for copy in entry_copies[:2] + wk_copies[:1]:
         copy.start()
 
-    below = rank + column
+    below = column + jnp.minimum(rank, 1)
 
     @pl.when(below > 0)
     def _():
@@ -109,12 +109,9 @@
                 near_sem.at[e - 1], inc=1, device_id=at_column(-e), device_id_type=MESH
             )
 
-    for d in range(1, groups):
-        @pl.when(rank >= d)
-        def _():
-            pl.semaphore_signal(
-                rank_sem, inc=1, device_id=at_group(-d), device_id_type=MESH
-            )
+    @pl.when(rank > 0)
+    def _():
+        pl.semaphore_signal(rank_sem, inc=1, device_id=(0, column), device_id_type=MESH)
 
     def remote(src, dst, send, recv, target):
         return pltpu.make_async_remote_copy(
@@ -340,9 +337,17 @@
                 mine_key[k] = rounded(fresh_rows(k))
 
         if c == cuts - 1:
-            @pl.when(rank < groups - 1)
+            @pl.when(rank == 0)
             def _():
-                pl.semaphore_wait(rank_sem, groups - 1 - rank)
+                pl.semaphore_wait(rank_sem, groups - 1)
+                for d in range(1, groups):
+                    pl.semaphore_signal(
+                        open_sem, inc=1, device_id=at_group(d), device_id_type=MESH
+                    )
+
+            @pl.when(rank > 0)
+            def _():
+                pl.semaphore_wait(open_sem, 1)
 
             for d in range(1, groups):
                 mine_copy(d).start()
@@ -443,7 +448,7 @@
 
         count = (high - low) * cut
         start = low * cut
-        lax.fori_loop(start, start + count, head, 0, unroll=min(count, 8))
+        lax.fori_loop(start, start + count, head, 0, unroll=True)
         for e in range(columns):
             for s in range(PAIR):
                 value = rounded(rows_out[pl.ds(place(0, e, s) + start, count)])
@@ -484,10 +489,21 @@
 
     for member in settled[1:]:
         attend(member)
+    odd = lax.rem(rank, 2) == 1
+    past = [jnp.where(odd, a, b) for a, b in zip(near_down[1:], far_down[:-1])]
     send_back(pieces_of(settled[1:], back_pieces), near_down[:1])
-    send_back(pieces_of(first[1:], back_pieces), far_down[:-1])
-    for e in far_down[:-1]:
-        send_back(pieces_of(rest, back_pieces), [e])
+    upper = jnp.logical_and(2 * column >= columns, jnp.logical_not(odd))
+
+    @pl.when(upper)
+    def _():
+        for e in past:
+            send_back(pieces_of(settled[1:], back_pieces), [e])
+
+    @pl.when(jnp.logical_not(upper))
+    def _():
+        send_back(pieces_of(first[1:], back_pieces), past)
+        for e in past:
+            send_back(pieces_of(rest, back_pieces), [e])
     wv_copy.wait()
     for member in moving:
         project(member, None)
@@ -585,6 +601,7 @@
             dma, dma((2 * units,)),
             dma, dma, dma, dma, dma, dma, dma, dma,
             pltpu.SemaphoreType.REGULAR((columns - 1,)), pltpu.SemaphoreType.REGULAR,
+            pltpu.SemaphoreType.REGULAR,
         ],
         compiler_params=pltpu.CompilerParams(
             collective_id=0, has_side_effects=True, vmem_limit_bytes=44 << 20

time: 56 us -> 55.2 us (0.986)
  Pallas kernels: 54.4 us -> 53.1 us
    pallas_call x1, Pallas kernels: 54.4 us -> 53.1 us  [body(): pl.pallas_call(functools.partial(kernel, groups, columns, scale), out_sha...]
where the time goes in v5:
time: 55.2 us; the launch traced here: 54.5 us
  Pallas kernels  53.1 us (96%)
  local copies, waits for them, and re-layouts  0.71 us (1%)
  between operations  0.66 us (1%)
    pallas_call x1, Pallas kernels, body(): pl.pallas_call(functools.partial(kernel, groups, columns, scale), out_sha...  53.1 us

profile of v5, /device:TPU:0, one launch (start us, length us, event | category | flops | bytes accessed | tf_op | source)
XLA Modules:
  0.0 54.5 jit_solution(1724520403251705511)
XLA Ops:
  0.7 53.1 %shard_map.82 = bf16[4,8,32,128]{3,2,1,0:T(8,128)(2,1)S(1)} custom-call(s32[64]{0:T(128)} %length_hbm.1, s32[1,1]{1,0:T(1,128)S(6)} %copy.11.move_ref, bf16[4,8,32,128]{3,2,1,0:T(8,128)(2,1)} %nope_hbm.1, bf16[4,8,32,64]{3,2,1,0:T(8,128)(2,1)} %rope_hbm.1, bf16[4,2,576]{2,1,0:T(2,128)(2,1)} %fresh_hbm.1, bf16[32,128,512]{2,1,0:T(8,128)(2,1)} %wk_hbm.1, ...), custom_call_target="tpu_custom_call" | custom-call | tf_op jit(solution)/shard_map/pallas_call | solution.py:564
  53.8 0.7 %copy.10 = bf16[4,8,32,128]{3,2,1,0:T(8,128)(2,1)} copy(bf16[4,8,32,128]{3,2,1,0:T(8,128)(2,1)S(1)} %shard_map.82) | data formatting | bytes 524288

commit v6 on v5

--- a/solution.py
+++ b/solution.py
@@ -65,17 +65,6 @@
     def at_group(d):
         return (lax.rem(rank + d + groups, groups), column)
 
-    barrier = pltpu.get_barrier_semaphore()
-    for e in range(1, columns):
-        @pl.when(column + e < columns)
-        def _():
-            pl.semaphore_signal(barrier, inc=1, device_id=at_column(e), device_id_type=MESH)
-
-    @pl.when(rank == 0)
-    def _():
-        for d in range(1, groups):
-            pl.semaphore_signal(barrier, inc=1, device_id=at_group(d), device_id_type=MESH)
-
     wk_copies = [
         pltpu.make_async_copy(
             wk_hbm.at[pl.ds(n * part, part)], wk.at[pl.ds(n * part, part)], local_sem.at[n]
@@ -96,6 +85,17 @@
     for copy in entry_copies[:2] + wk_copies[:1]:
         copy.start()
 
+    barrier = pltpu.get_barrier_semaphore()
+    for e in range(1, columns):
+        @pl.when(column + e < columns)
+        def _():
+            pl.semaphore_signal(barrier, inc=1, device_id=at_column(e), device_id_type=MESH)
+
+    @pl.when(rank == 0)
+    def _():
+        for d in range(1, groups):
+            pl.semaphore_signal(barrier, inc=1, device_id=at_group(d), device_id_type=MESH)
+
     below = column + jnp.minimum(rank, 1)
 
     @pl.when(below > 0)
@@ -140,6 +140,7 @@
         return remote(home, home_recv.at[d - 1], home_ss, home_rs, at_group(d))
 
     per = PAIR * cut
+    joined = max(cuts - 2, 0)
     others = pl.ds(1, columns - 1)
     halves = [(0, cuts - 1), (cuts - 1, cuts)] if cuts > 1 else [(0, 1)]
     back_pieces = {member: [(0, cuts)] for member in number}
@@ -151,7 +152,8 @@
         return pl.ds(piece[0] * per, (piece[1] - piece[0]) * per)
 
     def lat_copy(e, c):
-        return remote(lat_send.at[e, c], lat_recv.at[e, c], lat_ss, lat_rs, at_column(e))
+        at = pl.ds(c, cuts - c) if c == joined else pl.ds(c, 1)
+        return remote(lat_send.at[e, at], lat_recv.at[e, at], lat_ss, lat_rs, at_column(e))
 
     def late_copy(e):
         return remote(late_send.at[e], late_recv.at[e], late_ss, late_rs, at_column(e))
@@ -306,25 +308,25 @@
         return found
 
     def after_settled(c):
-        asked = 0
+        ready = [j for j in ([joined] if c == cuts - 1 else [c]) if j < joined or c == cuts - 1]
         for e in range(1, columns):
             @pl.when(column + e >= columns)
             def _():
-                lat_copy(e, c).start()
-
-            if c == asked:
+                for j in ready:
+                    lat_copy(e, j).start()
+
+            if c == 0:
                 @pl.when(column + e < columns)
                 def _():
                     pl.semaphore_wait(near_sem.at[e - 1], 1)
                     rot_copy(0, e).start()
                     shift_copy(e).start()
 
-        if c >= asked:
-            for e in range(1, columns):
-                @pl.when(column + e < columns)
-                def _():
-                    for j in range(c + 1) if c == asked else [c]:
-                        lat_copy(e, j).start()
+        for e in range(1, columns):
+            @pl.when(column + e < columns)
+            def _():
+                for j in ready:
+                    lat_copy(e, j).start()
 
         if c == 0:
             for copy in entry_copies[2:]:
@@ -410,7 +412,7 @@
         scores = jnp.concatenate([cached, decoded], axis=1)
         scores = jnp.where(token <= span * PAIR + within, scores * scale, -jnp.inf)
         spread = jnp.exp(scores - jnp.max(scores, axis=1, keepdims=True))
-        weights = rounded(spread / jnp.sum(spread, axis=1, keepdims=True))
+        weights = rounded(spread * (1.0 / jnp.sum(spread, axis=1, keepdims=True)))
         mixed = rounded(
             lax.dot_general(
                 weights[:, :capacity], keys[k, :latent], nt, preferred_element_type=jnp.float32

time: 55.2 us -> 54.9 us (level)
  no operation moved by 1% of the time
where the time goes in v6:
time: 54.9 us; the launch traced here: 54.5 us
  Pallas kernels  53.1 us (97%)
  local copies, waits for them, and re-layouts  0.71 us (1%)
  between operations  0.66 us (1%)
    pallas_call x1, Pallas kernels, body(): pl.pallas_call(functools.partial(kernel, groups, columns, scale), out_sha...  53.1 us

profile of v6, /device:TPU:0, one launch (start us, length us, event | category | flops | bytes accessed | tf_op | source)
XLA Modules:
  0.0 54.5 jit_solution(9522372758130560997)
XLA Ops:
  0.7 53.1 %shard_map.82 = bf16[4,8,32,128]{3,2,1,0:T(8,128)(2,1)S(1)} custom-call(s32[64]{0:T(128)} %length_hbm.1, s32[1,1]{1,0:T(1,128)S(6)} %copy.11.move_ref, bf16[4,8,32,128]{3,2,1,0:T(8,128)(2,1)} %nope_hbm.1, bf16[4,8,32,64]{3,2,1,0:T(8,128)(2,1)} %rope_hbm.1, bf16[4,2,576]{2,1,0:T(2,128)(2,1)} %fresh_hbm.1, bf16[32,128,512]{2,1,0:T(8,128)(2,1)} %wk_hbm.1, ...), custom_call_target="tpu_custom_call" | custom-call | tf_op jit(solution)/shard_map/pallas_call | solution.py:566
  53.8 0.7 %copy.10 = bf16[4,8,32,128]{3,2,1,0:T(8,128)(2,1)} copy(bf16[4,8,32,128]{3,2,1,0:T(8,128)(2,1)S(1)} %shard_map.82) | data formatting | bytes 524288
